TPU v7x, 128 devices: a whole 4x4x4 slice. The times are simulated.
128 devices in a mesh: blk: 8 (over z, x_lo), tp: 16 (over x_hi, y, core).
Axes of the slice: x: 4 (x_hi: 2, x_lo: 2; x = x_hi * 2 + x_lo), y: 4, z: 4, core: 2. Of those that a mesh axis runs over, the one named last changes fastest.
Arguments:
- input_pool: bfloat16 [4096, 1792], P(None, 'tp'), may hold values from -6 to 6
- teacher_pool: bfloat16 [4096, 1792], P(None, 'tp'), may hold values from -6 to 6
- gate_weight: bfloat16 [1792, 9472], P(None, 'tp'), may hold values from -0.125 to 0.125
- up_weight: bfloat16 [1792, 9472], P(None, 'tp'), may hold values from -0.125 to 0.125
- params: float32 [8, 9472, 1792], P('blk', 'tp'), may hold values from -6 to 6
- batch_ids: int32 [8, 1024], replicated, may hold values from 0 to 4095
- cycle_order: int32 [8], replicated, may hold values from 0 to 7, each once
- edge_weight: float32 [8], replicated, may hold values from 0.1 to 0.45
Outputs:
- updated: float32 [8, 9472, 1792], P('blk', 'tp')
Inputs may be any that keep to these rules, and one draw needn't show every extreme that they name: `cycle_order`: the 8 cycle positions name 8 different agents.
All inputs are finite; a program needn't handle non-finite values.
Results may differ from a plain program's by a relative error of at most 0.0061.
Values may be sent and summed in bfloat16 or wider, within the bound.
No kernel may reach another device: no remote copies, remote signals or barrier semaphores. Data moves between devices by JAX's collectives and lax.ppermute only.
A program may use at most 128 MiB of HBM per device.

v0:
```python
import jax
import jax.numpy as jnp
from jax import lax
from jax.sharding import PartitionSpec as P


def rows_first(arrays, axis, dims):
    turned = [jnp.moveaxis(a, dim, 0) for a, dim in zip(arrays, dims)]
    both = jnp.concatenate([t.reshape(len(t), -1) for t in turned], axis=1)
    out, at, finished = (lax.all_gather(both, axis, axis=0, tiled=True), 0, [])
    for t, dim in zip(turned, dims):
        slab = out[:, at : at + t[0].size].reshape(-1, *t.shape[1:])
        finished.append(jnp.moveaxis(slab, 0, dim))
        at += t[0].size
    return tuple(finished)


def shifted(array, axis, by):
    count = lax.axis_size(axis)
    return lax.ppermute(array, axis, [(i, (i + by) % count) for i in range(count)])


def body(
    input_pool, teacher_pool, gate_weight, up_weight, params, batch_ids, cycle_order, edge_weight
):
    step_rate = 2.0
    groups = lax.axis_size("tp")
    place = lax.axis_index("blk")
    agents = cycle_order.shape[0]
    slots = jnp.arange(agents, dtype=jnp.int32)
    here = slots == place
    before = slots == (place + agents - 1) % agents
    agent = jnp.sum(jnp.where(here, cycle_order, 0))
    weight_next = jnp.sum(jnp.where(here, edge_weight, 0.0))
    weight_prev = jnp.sum(jnp.where(before, edge_weight, 0.0))
    weight_self = 1.0 - weight_next - weight_prev
    batch = lax.dynamic_slice_in_dim(batch_ids, agent, 1, 0)[0]
    inputs_local = jnp.take(input_pool, batch, axis=0)
    teacher_local = jnp.take(teacher_pool, batch, axis=0)
    hidden_dev = gate_weight.shape[1]
    scale = float(hidden_dev * groups) ** (-0.5)
    pieces = rows_first((inputs_local, teacher_local), "tp", (1, 1))
    rows = pieces[0]
    gate = jnp.dot(rows, gate_weight, preferred_element_type=jnp.float32)
    up = jnp.dot(rows, up_weight, preferred_element_type=jnp.float32)
    teacher = pieces[1]
    gate, up, teacher_full = (gate, up, teacher)
    hidden = (jax.nn.silu(gate) * up).astype(jnp.bfloat16)

    def gradient(weights):
        weights_half = weights.astype(jnp.bfloat16)
        partial_out = scale * jnp.dot(hidden, weights_half, preferred_element_type=jnp.float32)
        output = lax.psum(partial_out, "tp")
        resid = (output - teacher_full.astype(jnp.float32)).astype(jnp.bfloat16)
        return scale * lax.dot_general(
            hidden, resid, (((0,), (0,)), ((), ())), preferred_element_type=jnp.float32
        )

    start_field = params[0]
    grad_first = gradient(start_field)

    def mix_two(field):
        lower = shifted(field.astype(jnp.bfloat16), "blk", 1).astype(field.dtype)
        upper = shifted(field.astype(jnp.bfloat16), "blk", -1).astype(field.dtype)
        return weight_self * field + weight_next * upper + weight_prev * lower

    moved = mix_two(start_field) - step_rate * grad_first
    combined = moved - step_rate * grad_first
    grad_second = gradient(moved)
    result = mix_two(combined) - step_rate * (grad_second - grad_first)
    return result[None]


def solution(mesh):
    placed = (
        P(None, "tp"),
        P(None, "tp"),
        P(None, "tp"),
        P(None, "tp"),
        P("blk", "tp", None),
        P(),
        P(),
        P(),
    )
    return jax.shard_map(
        body, mesh=mesh, in_specs=placed, out_specs=P("blk", "tp", None), check_vma=False
    )
```

profile of v0, /device:TPU:0, one launch (start us, length us, event | category | flops | bytes accessed | tf_op | source)
XLA Modules:
  0.0 552.1 jit_solution(8042731751094256005)
XLA Ops:
  6.5 0.0 copy-start
  6.5 0.0 all-gather.2.cloned.1.call-start
  6.5 1.4 fusion.20
  9.9 0.8 constant_dynamic-slice_fusion
  10.7 2.3 copy.11
  13.0 1.6 copy.12
  14.6 4.2 gather_fusion
  18.8 4.3 gather_fusion.1
  23.1 1.2 select_bitcast_fusion.1
  24.3 0.1 pad_maximum_fusion
  24.4 1.0 copy.13
  25.4 0.0 all-gather.2.cloned.1.call-update
  25.4 0.0 all-reduce.3.cloned.1.call-start
  25.5 3.7 convert_bitcast_fusion
  29.2 67.0 %all-gather.2.cloned.1.call-done = bf16[1792,2048]{1,0:T(8,128)(2,1)} async-done(((bf16[112,2048]{1,0:T(8,128)(2,1)}), bf16[1792,2048]{1,0:T(8,128)(2,1)}) %all-gather.2.cloned.1.call-update) | async-done | bytes 7340048 | tf_op jit(solution)/shard_map/all_gather | solution.py:10
  96.2 0.0 copy-done
  96.2 0.0 copy-start.5
  96.2 4.5 fusion.11
  100.7 0.0 copy-done.5
  100.7 0.2 copy-done.7
  101.0 0.0 copy-start.4
  101.0 2.6 multiply_convert_fusion
  103.5 0.0 copy-done.4
  103.5 5.2 convolution_multiply_fusion.1
  108.7 0.0 copy-start.6
  108.7 0.0 all-reduce.3.cloned.1.call-update
  108.7 0.0 all-reduce.5.cloned.1.call-start
  108.8 3.0 collective-permute-start
  111.8 0.0 collective-permute-start.1
  111.8 0.0 copy-done.6
  111.8 0.7 fusion.19
  113.8 65.8 %collective-permute-done = bf16[592,1792]{1,0:T(8,128)(2,1)S(1)} collective-permute-done((bf16[592,1792]{1,0:T(8,128)(2,1)}, bf16[592,1792]{1,0:T(8,128)(2,1)S(1)}, u32[]{:S(2)}, u32[]{:S(2)}) %collective-permute-start) | collective-permute-done | bytes 2121760 | tf_op jit(solution)/shard_map/ppermute | solution.py:20
  179.6 62.6 %collective-permute-done.1 = bf16[592,1792]{1,0:T(8,128)(2,1)} collective-permute-done((bf16[592,1792]{1,0:T(8,128)(2,1)}, bf16[592,1792]{1,0:T(8,128)(2,1)}, u32[]{:S(2)}, u32[]{:S(2)}) %collective-permute-start.1) | collective-permute-done | bytes 2121760 | tf_op jit(solution)/shard_map/ppermute | solution.py:20
  242.2 65.9 %all-reduce.3.cloned.1.call-done = f32[1024,1792]{0,1:T(8,128)} async-done(((f32[1024,1792]{0,1:T(8,128)}), f32[1024,1792]{0,1:T(8,128)}) %all-reduce.3.cloned.1.call-update) | async-done | bytes 7340048 | tf_op jit(solution)/shard_map/psum | solution.py:53
  308.1 13.2 %fusion.4 = (bf16[592,1792]{1,0:T(8,128)(2,1)}, f32[592,1792]{1,0:T(8,128)S(1)}, f32[592,1792]{1,0:T(8,128)}) fusion(bf16[592,1792]{1,0:T(8,128)(2,1)} %collective-permute-done.1, f32[]{:T(128)} %get-tuple-element.7, bf16[592,1792]{1,0:T(8,128)(2,1)S(1)} %collective-permute-done, f32[]{:T(128)} %get-tuple-element.6, f32[1,592,1792]{2,1,0:T(8,128)} %param.14, ...), kind=kOutput, calls=%fused_computation.13 | convolution fusion | flops 2189824000 | bytes 31319044 | tf_op jit(solution)/shard_map/dot_general | solution.py:55
  321.3 2.0 copy-done.2
  323.3 5.2 convolution_multiply_fusion
  328.5 0.0 all-reduce.5.cloned.1.call-update
  328.5 1.6 copy-done.3
  330.1 2.9 collective-permute-start.2
  333.0 0.0 collective-permute-start.3
  333.0 197.4 %all-reduce.5.cloned.1.call-done = f32[1024,1792]{0,1:T(8,128)} async-done(((f32[1024,1792]{0,1:T(8,128)}), f32[1024,1792]{0,1:T(8,128)}) %all-reduce.5.cloned.1.call-update) | async-done | bytes 7340048 | tf_op jit(solution)/shard_map/psum | solution.py:53
  530.5 6.6 %fusion.5 = f32[592,1792]{1,0:T(8,128)S(1)} fusion(bf16[1024,592]{0,1:T(8,128)(2,1)S(1)} %multiply_convert_fusion, f32[1024,1792]{0,1:T(8,128)} %all-reduce.5.cloned.1.call-done, bf16[1792,2048]{1,0:T(8,128)(2,1)} %all-gather.2.cloned.1.call-done), kind=kOutput, calls=%fused_computation.14 | convolution fusion | flops 2178154496 | bytes 16465920 | tf_op jit(solution)/shard_map/dot_general | solution.py:55
  537.0 0.0 collective-permute-done.2
  537.0 0.0 collective-permute-done.3
  537.0 0.0 copy-start.1
  537.1 8.5 %subtract_bitcast_fusion = f32[1,592,1792]{2,1,0:T(8,128)} fusion(f32[592,1792]{1,0:T(8,128)} %get-tuple-element.12, f32[592,1792]{1,0:T(8,128)S(1)} %fusion.5, bf16[592,1792]{1,0:T(8,128)(2,1)} %collective-permute-done.3, bf16[592,1792]{1,0:T(8,128)(2,1)} %collective-permute-done.2, f32[592,1792]{1,0:T(8,128)} %copy-done.2, f32[]{:T(128)} %get-tuple-element.7, ...), kind=kLoop, calls=%fused_computation.11 | loop fusion | flops 14852096 | bytes 21217292 | tf_op jit(solution)/shard_map/broadcast_in_dim | solution.py:71
  545.5 0.0 copy-done.1
  (5 shorter events, 0.0 us)
Async XLA Ops:
  6.5 89.6 %copy-start = (bf16[1792,592]{0,1:T(8,128)(2,1)S(1)}, bf16[1792,592]{0,1:T(8,128)(2,1)}, u32[]{:S(2)}) copy-start(bf16[1792,592]{0,1:T(8,128)(2,1)} %param.12) | copy-start | bytes 6365188
  6.5 89.6 %all-gather.2.cloned.1.call-start = ((), (), s32[]{:S(2)}) async-start(), calls=%async_computation | async-start | bytes 7798784 | tf_op jit(solution)/shard_map/all_gather | solution.py:10
  25.4 282.7 %all-reduce.3.cloned.1.call-start = ((), (), s32[]{:S(2)}) async-start(), calls=%async_computation.1 | async-start | bytes 14680064 | tf_op jit(solution)/shard_map/psum | solution.py:53
  96.2 4.5 copy-start.5
  96.2 4.8 copy-start.7
  101.0 2.6 copy-start.4
  108.7 3.1 copy-start.6
  108.7 421.7 %all-reduce.5.cloned.1.call-start = ((), (), s32[]{:S(2)}) async-start(), calls=%async_computation.2 | async-start | bytes 14680064 | tf_op jit(solution)/shard_map/psum | solution.py:53
  108.8 70.8 %collective-permute-start = (bf16[592,1792]{1,0:T(8,128)(2,1)}, bf16[592,1792]{1,0:T(8,128)(2,1)S(1)}, u32[]{:S(2)}, u32[]{:S(2)}) collective-permute-start(bf16[592,1792]{1,0:T(8,128)(2,1)} %convert_bitcast_fusion), channel_id=1, source_target_pairs={{0,112},{16,0},{32,16},{48,32},{64,48},{80,64},{96,80},{112,96},{1... | collective-permute-start | bytes 6365192 | tf_op jit(solution)/shard_map/ppermute | solution.py:20
  111.8 130.4 %collective-permute-start.1 = (bf16[592,1792]{1,0:T(8,128)(2,1)}, bf16[592,1792]{1,0:T(8,128)(2,1)}, u32[]{:S(2)}, u32[]{:S(2)}) collective-permute-start(bf16[592,1792]{1,0:T(8,128)(2,1)} %convert_bitcast_fusion), channel_id=1, source_target_pairs={{0,16},{16,32},{32,48},{48,64},{64,80},{80,96},{96,112},{112,0},{1... | collective-permute-start | bytes 6365192 | tf_op jit(solution)/shard_map/ppermute | solution.py:20
  321.3 2.0 copy-start.2
  328.5 1.6 copy-start.3
  330.1 206.9 %collective-permute-start.2 = (bf16[592,1792]{1,0:T(8,128)(2,1)S(1)}, bf16[592,1792]{1,0:T(8,128)(2,1)}, u32[]{:S(2)}, u32[]{:S(2)}) collective-permute-start(bf16[592,1792]{1,0:T(8,128)(2,1)S(1)} %copy-done.3), channel_id=1, source_target_pairs={{0,112},{16,0},{32,16},{48,32},{64,48},{80,64},{96,80},{112,96},{1... | collective-permute-start | bytes 6365192 | tf_op jit(solution)/shard_map/ppermute | solution.py:20
  333.0 204.0 %collective-permute-start.3 = (bf16[592,1792]{1,0:T(8,128)(2,1)S(1)}, bf16[592,1792]{1,0:T(8,128)(2,1)}, u32[]{:S(2)}, u32[]{:S(2)}) collective-permute-start(bf16[592,1792]{1,0:T(8,128)(2,1)S(1)} %copy-done.3), channel_id=1, source_target_pairs={{0,16},{16,32},{32,48},{48,64},{64,80},{80,96},{96,112},{112,0},{1... | collective-permute-start | bytes 6365192 | tf_op jit(solution)/shard_map/ppermute | solution.py:20
  537.0 8.5 %copy-start.1 = (bf16[1792,592]{0,1:T(8,128)(2,1)S(1)}, bf16[1792,592]{0,1:T(8,128)(2,1)}, u32[]{:S(2)}) copy-start(bf16[1792,592]{0,1:T(8,128)(2,1)} %param.12) | copy-start | bytes 6365188
Sparse Core Ops, SparseCore 0:
  25.5 70.5 all-gather.1
  108.9 199.2 all-reduce.2
  328.6 201.7 all-reduce.4
where the time goes:
time: 553 us; the launch traced here: 552 us
  waiting for transfers between devices  459 us (83%)
  matrix products  37.1 us (7%)
  local copies, waits for them, and re-layouts  18 us (3%)
  between operations  16.5 us (3%)
  other arithmetic  15.6 us (3%)
  starting transfers between devices  6.06 us (1%)
    psum x2, waiting for transfers between devices, gradient(): output = lax.psum(partial_out, 'tp')  263 us
    ppermute x4, waiting for transfers between devices, shifted(): lax.ppermute(array, axis, [(i, (i + by) % count) for i in range(count)])  128 us
    all_gather x1, waiting for transfers between devices, rows_first(): out, at, finished = (lax.all_gather(both, axis, axis=0, tiled=True), 0, [])  67 us
    dot_general x2, matrix products, gradient(): lax.dot_general(hidden, resid, (((0,), (0,)), ((), ())), preferred_elemen...  19.7 us
  transfers between devices with their start and end apart: 7, of which 5 were waited for; matrix products, arithmetic and copies ran while one was open for 2% of the time, Pallas kernels for 0%

commit v1 on v0

--- a/solution.py
+++ b/solution.py
@@ -7,7 +7,13 @@
 def rows_first(arrays, axis, dims):
     turned = [jnp.moveaxis(a, dim, 0) for a, dim in zip(arrays, dims)]
     both = jnp.concatenate([t.reshape(len(t), -1) for t in turned], axis=1)
-    out, at, finished = (lax.all_gather(both, axis, axis=0, tiled=True), 0, [])
+    out, at, finished = (
+        jnp.concatenate(
+            lax.all_to_all(jnp.stack([both] * lax.axis_size(axis)), axis, 0, 0), axis=0
+        ),
+        0,
+        [],
+    )
     for t, dim in zip(turned, dims):
         slab = out[:, at : at + t[0].size].reshape(-1, *t.shape[1:])
         finished.append(jnp.moveaxis(slab, 0, dim))

time: 553 us -> 610 us (1.10)
  waiting for transfers between devices: 459 us -> 504 us
  starting transfers between devices: 6.06 us -> 12.3 us
    all_to_all x0 -> x1, waiting for transfers between devices: none -> 101 us  [rows_first(): lax.all_to_all(jnp.stack([both] * lax.axis_size(axis)), axis, 0, 0)]
    all_gather x1 -> x0, waiting for transfers between devices: 67 us -> none  [rows_first(): out, at, finished = (lax.all_gather(both, axis, axis=0, tiled=True), 0, [])]
    psum x2, waiting for transfers between devices: 263 us -> 274 us  [gradient(): output = lax.psum(partial_out, 'tp')]
    all_to_all x0 -> x1, starting transfers between devices: none -> 7.19 us  [rows_first(): lax.all_to_all(jnp.stack([both] * lax.axis_size(axis)), axis, 0, 0)]
where the time goes in v1:
time: 610 us; the launch traced here: 609 us
  waiting for transfers between devices  504 us (83%)
  matrix products  39.3 us (6%)
  local copies, waits for them, and re-layouts  21 us (3%)
  between operations  16.7 us (3%)
  other arithmetic  15.5 us (3%)
  starting transfers between devices  12.3 us (2%)
    psum x2, waiting for transfers between devices, gradient(): output = lax.psum(partial_out, 'tp')  274 us
    ppermute x4, waiting for transfers between devices, shifted(): lax.ppermute(array, axis, [(i, (i + by) % count) for i in range(count)])  130 us
    all_to_all x1, waiting for transfers between devices, rows_first(): lax.all_to_all(jnp.stack([both] * lax.axis_size(axis)), axis, 0, 0)  101 us
    dot_general x2, matrix products, gradient(): lax.dot_general(hidden, resid, (((0,), (0,)), ((), ())), preferred_elemen...  19.7 us
  transfers between devices with their start and end apart: 7, of which 5 were waited for; matrix products, arithmetic and copies ran while one was open for 2% of the time, Pallas kernels for 0%

profile of v1, /device:TPU:0, one launch (start us, length us, event | category | flops | bytes accessed | tf_op | source)
XLA Modules:
  0.0 609.1 jit_solution(6898746920318463987)
XLA Ops:
  6.5 0.0 copy-start
  6.5 1.4 fusion.20
  9.9 0.8 constant_dynamic-slice_fusion
  10.7 2.3 copy.9
  13.0 1.6 copy.10
  14.6 4.2 gather_fusion
  18.8 4.3 gather_fusion.1
  23.1 1.2 select_bitcast_fusion.1
  24.3 0.1 pad_maximum_fusion
  24.4 0.2 copy.11
  24.6 3.9 stack.2
  28.6 7.2 %all-to-all-start = ((bf16[16,112,2048]{2,1,0:T(8,128)(2,1)}), bf16[16,112,2048]{2,1,0:T(8,128)(2,1)}, u32[]{:S(2)}, u32[]{:S(2)}) async-start(bf16[16,112,2048]{2,1,0:T(8,128)(2,1)} %stack.2), calls=%async_computation | async-start | bytes 14680064 | tf_op jit(solution)/shard_map/all_to_all | solution.py:12
  35.8 0.0 all-reduce.3.cloned.1.call-start
  35.8 3.7 convert_bitcast_fusion
  39.6 100.5 %all-to-all-done = bf16[16,112,2048]{2,1,0:T(8,128)(2,1)} async-done(((bf16[16,112,2048]{2,1,0:T(8,128)(2,1)}), bf16[16,112,2048]{2,1,0:T(8,128)(2,1)}, u32[]{:S(2)}, u32[]{:S(2)}) %all-to-all-start) | async-done | bytes 7340064 | tf_op jit(solution)/shard_map/all_to_all | solution.py:12
  140.1 0.0 copy-done
  140.1 0.0 copy-start.6
  140.1 4.5 fusion.11
  144.6 0.0 copy-done.6
  144.6 0.0 copy-start.4
  144.7 4.8 multiply_convert_fusion
  149.4 0.0 copy-done.4
  149.5 5.2 convolution_multiply_fusion.1
  154.6 0.0 copy-start.5
  154.6 0.0 all-reduce.3.cloned.1.call-update
  154.7 0.0 all-reduce.5.cloned.1.call-start
  154.7 0.1 collective-permute-start
  154.8 2.0 collective-permute-start.1
  156.8 0.0 copy-done.5
  156.8 0.7 fusion.19
  158.7 59.9 %collective-permute-done = bf16[592,1792]{1,0:T(8,128)(2,1)S(1)} collective-permute-done((bf16[592,1792]{1,0:T(8,128)(2,1)}, bf16[592,1792]{1,0:T(8,128)(2,1)S(1)}, u32[]{:S(2)}, u32[]{:S(2)}) %collective-permute-start) | collective-permute-done | bytes 2121760 | tf_op jit(solution)/shard_map/ppermute | solution.py:26
  218.7 70.0 %collective-permute-done.1 = bf16[592,1792]{1,0:T(8,128)(2,1)} collective-permute-done((bf16[592,1792]{1,0:T(8,128)(2,1)}, bf16[592,1792]{1,0:T(8,128)(2,1)}, u32[]{:S(2)}, u32[]{:S(2)}) %collective-permute-start.1) | collective-permute-done | bytes 2121760 | tf_op jit(solution)/shard_map/ppermute | solution.py:26
  288.6 76.3 %all-reduce.3.cloned.1.call-done = f32[1024,1792]{0,1:T(8,128)} async-done(((f32[1024,1792]{0,1:T(8,128)}), f32[1024,1792]{0,1:T(8,128)}) %all-reduce.3.cloned.1.call-update) | async-done | bytes 7340048 | tf_op jit(solution)/shard_map/psum | solution.py:59
  365.0 13.1 %fusion.4 = (bf16[592,1792]{1,0:T(8,128)(2,1)}, f32[592,1792]{1,0:T(8,128)S(1)}, f32[592,1792]{1,0:T(8,128)}) fusion(bf16[592,1792]{1,0:T(8,128)(2,1)} %collective-permute-done.1, f32[]{:T(128)} %get-tuple-element.7, bf16[592,1792]{1,0:T(8,128)(2,1)S(1)} %collective-permute-done, f32[]{:T(128)} %get-tuple-element.6, f32[1,592,1792]{2,1,0:T(8,128)} %param.14, ...), kind=kOutput, calls=%fused_computation.13 | convolution fusion | flops 2189824000 | bytes 31319044 | tf_op jit(solution)/shard_map/dot_general | solution.py:61
  378.1 0.0 copy-start.2
  378.1 2.0 copy-done.2
  380.1 5.2 convolution_multiply_fusion
  385.3 0.0 all-reduce.5.cloned.1.call-update
  385.3 1.6 copy-done.3
  386.9 3.0 collective-permute-start.2
  389.8 0.0 collective-permute-start.3
  389.8 197.4 %all-reduce.5.cloned.1.call-done = f32[1024,1792]{0,1:T(8,128)} async-done(((f32[1024,1792]{0,1:T(8,128)}), f32[1024,1792]{0,1:T(8,128)}) %all-reduce.5.cloned.1.call-update) | async-done | bytes 7340048 | tf_op jit(solution)/shard_map/psum | solution.py:59
  587.3 6.6 %fusion.5 = f32[592,1792]{1,0:T(8,128)S(1)} fusion(bf16[1024,592]{0,1:T(8,128)(2,1)S(1)} %multiply_convert_fusion, f32[1024,1792]{0,1:T(8,128)} %all-reduce.5.cloned.1.call-done, bf16[1792,2048]{1,0:T(8,128)(2,1)} %bitcast.5), kind=kOutput, calls=%fused_computation.14 | convolution fusion | flops 2178154496 | bytes 16465920 | tf_op jit(solution)/shard_map/dot_general | solution.py:61
  593.8 0.0 collective-permute-done.2
  593.8 0.0 collective-permute-done.3
  593.8 0.0 copy-start.1
  593.9 8.4 %subtract_bitcast_fusion = f32[1,592,1792]{2,1,0:T(8,128)} fusion(f32[592,1792]{1,0:T(8,128)} %get-tuple-element.12, f32[592,1792]{1,0:T(8,128)S(1)} %fusion.5, bf16[592,1792]{1,0:T(8,128)(2,1)} %collective-permute-done.3, bf16[592,1792]{1,0:T(8,128)(2,1)} %collective-permute-done.2, f32[592,1792]{1,0:T(8,128)} %copy-done.2, f32[]{:T(128)} %get-tuple-element.7, ...), kind=kLoop, calls=%fused_computation.11 | loop fusion | flops 14852096 | bytes 21217292 | tf_op jit(solution)/shard_map/broadcast_in_dim | solution.py:77
  602.3 0.0 copy-done.1
  (3 shorter events, 0.0 us)
Async XLA Ops:
  6.5 133.6 %copy-start = (bf16[1792,592]{0,1:T(8,128)(2,1)S(1)}, bf16[1792,592]{0,1:T(8,128)(2,1)}, u32[]{:S(2)}) copy-start(bf16[1792,592]{0,1:T(8,128)(2,1)} %param.12) | copy-start | bytes 6365188
  28.6 111.5 %all-to-all-start = ((bf16[16,112,2048]{2,1,0:T(8,128)(2,1)}), bf16[16,112,2048]{2,1,0:T(8,128)(2,1)}, u32[]{:S(2)}, u32[]{:S(2)}) async-start(bf16[16,112,2048]{2,1,0:T(8,128)(2,1)} %stack.2), calls=%async_computation | async-start | bytes 14680064 | tf_op jit(solution)/shard_map/all_to_all | solution.py:12
  35.8 329.2 %all-reduce.3.cloned.1.call-start = ((), (), s32[]{:S(2)}) async-start(), calls=%async_computation.1 | async-start | bytes 14680064 | tf_op jit(solution)/shard_map/psum | solution.py:59
  140.1 4.5 copy-start.6
  144.6 4.8 copy-start.4
  154.6 2.2 copy-start.5
  154.7 432.6 %all-reduce.5.cloned.1.call-start = ((), (), s32[]{:S(2)}) async-start(), calls=%async_computation.2 | async-start | bytes 14680064 | tf_op jit(solution)/shard_map/psum | solution.py:59
  154.7 63.9 %collective-permute-start = (bf16[592,1792]{1,0:T(8,128)(2,1)}, bf16[592,1792]{1,0:T(8,128)(2,1)S(1)}, u32[]{:S(2)}, u32[]{:S(2)}) collective-permute-start(bf16[592,1792]{1,0:T(8,128)(2,1)} %convert_bitcast_fusion), channel_id=1, source_target_pairs={{0,112},{16,0},{32,16},{48,32},{64,48},{80,64},{96,80},{112,96},{1... | collective-permute-start | bytes 6365192 | tf_op jit(solution)/shard_map/ppermute | solution.py:26
  154.8 133.8 %collective-permute-start.1 = (bf16[592,1792]{1,0:T(8,128)(2,1)}, bf16[592,1792]{1,0:T(8,128)(2,1)}, u32[]{:S(2)}, u32[]{:S(2)}) collective-permute-start(bf16[592,1792]{1,0:T(8,128)(2,1)} %convert_bitcast_fusion), channel_id=1, source_target_pairs={{0,16},{16,32},{32,48},{48,64},{64,80},{80,96},{96,112},{112,0},{1... | collective-permute-start | bytes 6365192 | tf_op jit(solution)/shard_map/ppermute | solution.py:26
  378.1 2.0 copy-start.2
  385.3 1.6 copy-start.3
  386.9 206.9 %collective-permute-start.2 = (bf16[592,1792]{1,0:T(8,128)(2,1)S(1)}, bf16[592,1792]{1,0:T(8,128)(2,1)}, u32[]{:S(2)}, u32[]{:S(2)}) collective-permute-start(bf16[592,1792]{1,0:T(8,128)(2,1)S(1)} %copy-done.3), channel_id=1, source_target_pairs={{0,112},{16,0},{32,16},{48,32},{64,48},{80,64},{96,80},{112,96},{1... | collective-permute-start | bytes 6365192 | tf_op jit(solution)/shard_map/ppermute | solution.py:26
  389.8 204.0 %collective-permute-start.3 = (bf16[592,1792]{1,0:T(8,128)(2,1)S(1)}, bf16[592,1792]{1,0:T(8,128)(2,1)}, u32[]{:S(2)}, u32[]{:S(2)}) collective-permute-start(bf16[592,1792]{1,0:T(8,128)(2,1)S(1)} %copy-done.3), channel_id=1, source_target_pairs={{0,16},{16,32},{32,48},{48,64},{64,80},{80,96},{96,112},{112,0},{1... | collective-permute-start | bytes 6365192 | tf_op jit(solution)/shard_map/ppermute | solution.py:26
  593.8 8.4 %copy-start.1 = (bf16[1792,592]{0,1:T(8,128)(2,1)S(1)}, bf16[1792,592]{0,1:T(8,128)(2,1)}, u32[]{:S(2)}) copy-start(bf16[1792,592]{0,1:T(8,128)(2,1)} %param.12) | copy-start | bytes 6365188
Sparse Core Ops, SparseCore 0:
  154.8 210.1 all-reduce.2
  385.4 201.7 all-reduce.4
